TPU v7x, 32 devices: a whole 2x2x4 slice. The times are simulated.
32 devices in a mesh: dp: 8 (over y, x, core), tensor: 4 (over z).
Axes of the slice: x: 2, y: 2, z: 4, core: 2. Of those that a mesh axis runs over, the one named last changes fastest.
Arguments:
- inputs: bfloat16 [32768, 768], P('dp'), may hold values from -6 to 6
- segments: int32 [64, 512], P('dp'), may hold values from 0 to 7, never falling along the last dimension, each value on 1 to 128 neighbouring positions
- w_query: bfloat16 [768, 768], P(None, 'tensor'), may hold values from -0.21875 to 0.21875
- w_key: bfloat16 [768, 768], P(None, 'tensor'), may hold values from -0.21875 to 0.21875
- w_value: bfloat16 [768, 768], P(None, 'tensor'), may hold values from -0.21875 to 0.21875
- b_query: bfloat16 [768], P('tensor'), may hold values from -3 to 3
- b_value: bfloat16 [768], P('tensor'), may hold values from -3 to 3
- w_output: bfloat16 [768, 768], P('tensor'), may hold values from -0.875 to 0.875
- b_output: bfloat16 [768], replicated, may hold values from -3 to 3
- gain_attn: bfloat16 [768], replicated, may hold values from 0.5 to 1.5
- shift_attn: bfloat16 [768], replicated, may hold values from -3 to 3
- w_hidden: bfloat16 [768, 3072], P(None, 'tensor'), may hold values from -0.21875 to 0.21875
- b_hidden: bfloat16 [3072], P('tensor'), may hold values from -3 to 3
- w_project: bfloat16 [3072, 768], P('tensor'), may hold values from -0.109375 to 0.109375
- b_project: bfloat16 [768], replicated, may hold values from -3 to 3
- gain_ffn: bfloat16 [768], replicated, may hold values from 0.5 to 1.5
- shift_ffn: bfloat16 [768], replicated, may hold values from -3 to 3
- cotangent: bfloat16 [32768, 768], P(('dp', 'tensor')), may hold values from -6 to 6
Outputs:
- output: bfloat16 [32768, 768], P(('dp', 'tensor'))
- grad_input: float32 [32768, 768], P(('dp', 'tensor'))
- grad_w_query: float32 [768, 768], P('dp', 'tensor')
- grad_w_key: float32 [768, 768], P('dp', 'tensor')
- grad_w_value: float32 [768, 768], P('dp', 'tensor')
- grad_w_output: float32 [768, 768], P('tensor', 'dp')
- grad_w_hidden: float32 [768, 3072], P('dp', 'tensor')
- grad_w_project: float32 [3072, 768], P('tensor', 'dp')
- grad_bias_qv: float32 [2, 12, 64], P(None, 'tensor', 'dp')
- grad_b_hidden: float32 [48, 64], P('tensor', 'dp')
- grad_vectors: float32 [6, 768], P(None, ('dp', 'tensor'))
Inputs may be any that keep to these rules, and one draw needn't show every extreme that they name: `segments`: within each row of 512 tokens segment numbers never fall; each text holds 1 to 128 tokens, and some text holds exactly 128.
All inputs are finite; a program needn't handle non-finite values.
Results may differ from a plain program's by a relative error of at most 0.014.
Values may be sent and summed in bfloat16 or wider, within the bound.
A program may use at most 192 MiB of HBM per device.

v0:
```python
import jax
import jax.numpy as jnp
from jax import lax
from jax.sharding import PartitionSpec as P

HD = 64


norm_epsilon = 1e-12
root_half = 0.7071067811865476


def norm_forward(values, norm_gain, norm_shift):
    average = jnp.mean(values, axis=-1, keepdims=True)
    centered = values - average
    variance = jnp.mean(centered * centered, axis=-1, keepdims=True)
    inverse = lax.rsqrt(variance + norm_epsilon)
    scaled = centered * inverse
    return (scaled * norm_gain + norm_shift, scaled, inverse)


def norm_backward(grad_out, scaled, inverse, norm_gain):
    weighted = grad_out * norm_gain
    mean_grad = jnp.mean(weighted, axis=-1, keepdims=True)
    mean_proj = jnp.mean(weighted * scaled, axis=-1, keepdims=True)
    return inverse * (weighted - mean_grad - scaled * mean_proj)


def gelu_exact(values):
    return 0.5 * values * (1.0 + lax.erf(values * root_half))


def cross_rows(left, right):
    return lax.dot_general(
        left, right, (((0,), (0,)), ((), ())), preferred_element_type=jnp.float32
    )


def times_transposed(left, right):
    return lax.dot_general(
        left, right, (((1,), (1,)), ((), ())), preferred_element_type=jnp.float32
    )


def masked_scores(queries, keys_in, segment_row):
    same_text = segment_row[:, None] == segment_row[None, :]
    scores = jnp.einsum("qhd,khd->hqk", queries, keys_in, preferred_element_type=jnp.float32)
    scores = scores * queries.shape[2] ** (-0.5)
    return jnp.where(same_text[None], scores, -1000000000.0)


def attend_forward(packed):
    queries, keys_in, values, segment_row = packed
    scores = masked_scores(queries, keys_in, segment_row)
    row_max = jnp.max(scores, axis=-1, keepdims=True)
    exponent = jnp.exp(scores - row_max)
    row_total = jnp.sum(exponent, axis=-1, keepdims=True)
    attn_probs = (exponent / row_total).astype(jnp.bfloat16)
    mixed_heads = jnp.einsum("hqk,khd->qhd", attn_probs, values, preferred_element_type=jnp.float32)
    return (mixed_heads.astype(jnp.bfloat16), row_max + jnp.log(row_total))


def attend_backward(packed):
    queries, keys_in, values, segment_row, logsum, grad_mixed = packed
    score_scale = queries.shape[2] ** (-0.5)
    scores = masked_scores(queries, keys_in, segment_row)
    attn_probs = jnp.exp(scores - logsum)
    grad_probs = jnp.einsum("qhd,khd->hqk", grad_mixed, values, preferred_element_type=jnp.float32)
    grad_values = jnp.einsum(
        "hqk,qhd->khd",
        attn_probs.astype(jnp.bfloat16),
        grad_mixed,
        preferred_element_type=jnp.float32,
    )
    inner_sum = jnp.sum(attn_probs * grad_probs, axis=-1, keepdims=True)
    grad_scores = (attn_probs * (grad_probs - inner_sum)).astype(jnp.bfloat16)
    grad_queries = (
        jnp.einsum("hqk,khd->qhd", grad_scores, keys_in, preferred_element_type=jnp.float32)
        * score_scale
    )
    grad_keys = (
        jnp.einsum("hqk,qhd->khd", grad_scores, queries, preferred_element_type=jnp.float32)
        * score_scale
    )
    return (
        grad_queries.astype(jnp.bfloat16),
        grad_keys.astype(jnp.bfloat16),
        grad_values.astype(jnp.bfloat16),
    )


def per_device(
    inputs,
    segments,
    w_query,
    w_key,
    w_value,
    b_query,
    b_value,
    w_output,
    b_output,
    gain_attn,
    shift_attn,
    w_hidden,
    b_hidden,
    w_project,
    b_project,
    gain_ffn,
    shift_ffn,
    cotangent,
):
    seq_len = segments.shape[1]
    row_count = segments.shape[0]
    token_count = inputs.shape[0]
    share_rows = cotangent.shape[0]
    offset = lax.axis_index("tensor") * share_rows
    head_width = w_query.shape[1]
    head_shape = (row_count, seq_len, head_width // HD, HD)
    attn_gain = gain_attn.astype(jnp.float32)
    attn_shift = shift_attn.astype(jnp.float32)
    attn_bias = b_output.astype(jnp.float32)
    ffn_gain = gain_ffn.astype(jnp.float32)
    ffn_shift = shift_ffn.astype(jnp.float32)
    ffn_bias = b_project.astype(jnp.float32)
    grad_out = cotangent.astype(jnp.float32)
    queries = (
        jnp.dot(inputs, w_query, preferred_element_type=jnp.float32) + b_query.astype(jnp.float32)
    ).astype(jnp.bfloat16)
    keys_in = jnp.dot(inputs, w_key, preferred_element_type=jnp.float32).astype(jnp.bfloat16)
    values = (
        jnp.dot(inputs, w_value, preferred_element_type=jnp.float32) + b_value.astype(jnp.float32)
    ).astype(jnp.bfloat16)
    query_heads = queries.reshape(head_shape)
    key_heads = keys_in.reshape(head_shape)
    value_heads = values.reshape(head_shape)
    mixed_heads, logsum = lax.map(attend_forward, (query_heads, key_heads, value_heads, segments))
    mixed_flat = mixed_heads.reshape(token_count, head_width)
    picked = mixed_flat
    branch_share = lax.psum_scatter(
        jnp.dot(picked, w_output, preferred_element_type=jnp.float32),
        "tensor",
        scatter_dimension=0,
        tiled=True,
    )
    input_share = lax.dynamic_slice_in_dim(inputs, offset, share_rows, 0).astype(jnp.float32)
    hidden_share = input_share + (branch_share + attn_bias)
    hidden_all = lax.all_gather(hidden_share, "tensor", axis=0, tiled=True)
    normed_all, scaled_all, inverse_all = norm_forward(hidden_all, attn_gain, attn_shift)
    normed_low = normed_all.astype(jnp.bfloat16)
    normed_share = lax.dynamic_slice_in_dim(normed_all, offset, share_rows, 0)
    scaled_share = lax.dynamic_slice_in_dim(scaled_all, offset, share_rows, 0)
    hidden_pre = jnp.dot(
        normed_low, w_hidden, preferred_element_type=jnp.float32
    ) + b_hidden.astype(jnp.float32)
    active, gelu_pull = jax.vjp(gelu_exact, hidden_pre)
    active_low = active.astype(jnp.bfloat16)
    picked = active_low
    second_share = lax.psum_scatter(
        jnp.dot(picked, w_project, preferred_element_type=jnp.float32),
        "tensor",
        scatter_dimension=0,
        tiled=True,
    )
    block_sum = normed_share + (second_share + ffn_bias)
    output_share, scaled_out, inverse_out = norm_forward(block_sum, ffn_gain, ffn_shift)
    grad_sum = norm_backward(grad_out, scaled_out, inverse_out, ffn_gain)
    grad_ffn_gain = jnp.sum(grad_out * scaled_out, axis=0)
    grad_ffn_shift = jnp.sum(grad_out, axis=0)
    grad_sum_low = grad_sum.astype(jnp.bfloat16)
    grad_ffn_bias = jnp.sum(grad_sum_low.astype(jnp.float32), axis=0)
    grad_sum_all = lax.all_gather(grad_sum_low, "tensor", axis=0, tiled=True)
    grad_active = times_transposed(grad_sum_all, w_project)
    grad_w_project = cross_rows(active_low, grad_sum_all)
    grad_hidden_pre = gelu_pull(grad_active)[0].astype(jnp.bfloat16)
    grad_b_hidden = jnp.sum(grad_hidden_pre.astype(jnp.float32), axis=0).reshape(-1, HD)
    grad_w_hidden = cross_rows(normed_low, grad_hidden_pre)
    picked = grad_hidden_pre
    grad_normed_share = grad_sum + lax.psum_scatter(
        times_transposed(picked, w_hidden), "tensor", scatter_dimension=0, tiled=True
    )
    grad_normed_all = lax.all_gather(grad_normed_share, "tensor", axis=0, tiled=True)
    grad_hidden_all = norm_backward(grad_normed_all, scaled_all, inverse_all, attn_gain)
    grad_hidden_share = lax.dynamic_slice_in_dim(grad_hidden_all, offset, share_rows, 0)
    grad_hidden_low = grad_hidden_all.astype(jnp.bfloat16)
    grad_attn_gain = jnp.sum(grad_normed_share * scaled_share, axis=0)
    grad_attn_shift = jnp.sum(grad_normed_share, axis=0)
    grad_attn_bias = jnp.sum(grad_hidden_share.astype(jnp.bfloat16).astype(jnp.float32), axis=0)
    grad_w_output = cross_rows(mixed_flat, grad_hidden_low)
    grad_mixed = (
        times_transposed(grad_hidden_low, w_output).astype(jnp.bfloat16).reshape(head_shape)
    )
    grad_query_heads, grad_key_heads, grad_value_heads = lax.map(
        attend_backward, (query_heads, key_heads, value_heads, segments, logsum, grad_mixed)
    )
    grad_queries = grad_query_heads.reshape(token_count, head_width)
    grad_keys = grad_key_heads.reshape(token_count, head_width)
    grad_values = grad_value_heads.reshape(token_count, head_width)
    grad_w_query = cross_rows(inputs, grad_queries)
    grad_w_key = cross_rows(inputs, grad_keys)
    grad_w_value = cross_rows(inputs, grad_values)
    grad_b_query = jnp.sum(grad_queries.astype(jnp.float32), axis=0)
    grad_b_value = jnp.sum(grad_values.astype(jnp.float32), axis=0)
    grad_bias_qv = jnp.stack([grad_b_query, grad_b_value]).reshape(2, head_width // HD, HD)
    summed = times_transposed(grad_queries, w_query)
    summed = summed + times_transposed(grad_keys, w_key)
    grad_input = grad_hidden_share + lax.psum_scatter(
        (summed + times_transposed(grad_values, w_value)).astype(jnp.bfloat16),
        "tensor",
        scatter_dimension=0,
        tiled=True,
    ).astype(jnp.float32)
    all_parts = (
        lax.psum_scatter(grad_w_query, "dp", scatter_dimension=0, tiled=True),
        lax.psum_scatter(grad_w_key, "dp", scatter_dimension=0, tiled=True),
        lax.psum_scatter(grad_w_value, "dp", scatter_dimension=0, tiled=True),
        lax.psum_scatter(grad_w_output, "dp", scatter_dimension=1, tiled=True),
        lax.psum_scatter(grad_w_hidden, "dp", scatter_dimension=0, tiled=True),
        lax.psum_scatter(grad_w_project, "dp", scatter_dimension=1, tiled=True),
        lax.psum_scatter(grad_bias_qv, "dp", scatter_dimension=2, tiled=True),
        lax.psum_scatter(grad_b_hidden, "dp", scatter_dimension=1, tiled=True),
    )
    (
        sum_query,
        sum_key,
        sum_value,
        sum_output,
        sum_hidden,
        sum_project,
        sum_bias_qv,
        sum_b_hidden,
    ) = all_parts
    vector_stack = jnp.stack(
        [
            grad_attn_gain,
            grad_attn_shift,
            grad_attn_bias,
            grad_ffn_gain,
            grad_ffn_shift,
            grad_ffn_bias,
        ]
    )
    sum_vectors = lax.psum_scatter(vector_stack, ("dp", "tensor"), scatter_dimension=1, tiled=True)
    return (
        output_share.astype(jnp.bfloat16),
        grad_input,
        sum_query,
        sum_key,
        sum_value,
        sum_output,
        sum_hidden,
        sum_project,
        sum_bias_qv,
        sum_b_hidden,
        sum_vectors,
    )


def solution(mesh):
    in_specs = (
        P("dp", None),
        P("dp", None),
        P(None, "tensor"),
        P(None, "tensor"),
        P(None, "tensor"),
        P("tensor"),
        P("tensor"),
        P("tensor", None),
        P(),
        P(),
        P(),
        P(None, "tensor"),
        P("tensor"),
        P("tensor", None),
        P(),
        P(),
        P(),
        P(("dp", "tensor"), None),
    )
    out_specs = (
        P(("dp", "tensor"), None),
        P(("dp", "tensor"), None),
        P("dp", "tensor"),
        P("dp", "tensor"),
        P("dp", "tensor"),
        P("tensor", "dp"),
        P("dp", "tensor"),
        P("tensor", "dp"),
        P(None, "tensor", "dp"),
        P("tensor", "dp"),
        P(None, ("dp", "tensor")),
    )
    return jax.shard_map(
        per_device, mesh=mesh, in_specs=in_specs, out_specs=out_specs, check_vma=False
    )
```

profile of v0, /device:TPU:0, one launch (start us, length us, event | category | flops | bytes accessed | tf_op | source)
XLA Modules:
  0.0 1853.3 jit_solution(15079120562952520668)
XLA Ops:
  8.7 5.0 fusion.54
  26.3 48.8 %while.26 = (s32[]{:T(128)}, bf16[8,512,3,64]{1,3,2,0:T(8,128)(2,1)}, f32[8,3,512,1]{2,1,3,0:T(4,128)S(1)}, bf16[8,512,3,64]{1,3,2,0:T(8,128)(2,1)}, s32[8,512]{...) while((s32[]{:T(128)}, ...), condition=%wide.region_3.4_spmd, body=%wide.region_0.3_spmd.sunk | while | flops 211122688 | bytes 11335781 | solution.py:136
  29.8 2.7 fusion.138
  35.9 2.7 fusion.138
  42.0 2.7 fusion.138
  48.0 2.7 fusion.138
  54.1 2.7 fusion.138
  60.2 2.7 fusion.138
  66.2 2.7 fusion.138
  72.3 2.7 fusion.138
  75.0 2.9 copy.70
  78.6 6.4 fusion.79
  85.7 214.1 %reduce-scatter.22.cloned.1.call-done = f32[1024,768]{1,0:T(8,128)} async-done(((f32[4096,768]{1,0:T(8,128)}), f32[1024,768]{1,0:T(8,128)}) %reduce-scatter.22.cloned.1.call-update) | async-done | bytes 3145744 | tf_op jit(solution)/shard_map/reduce_scatter | solution.py:139
  299.8 4.3 add_add_fusion.1
  304.9 218.7 %all-gather.4.cloned.1.call-done = f32[4096,768]{1,0:T(8,128)} async-done(((f32[1024,768]{1,0:T(8,128)}), f32[4096,768]{1,0:T(8,128)}) %all-gather.4.cloned.1.call-update) | async-done | bytes 12582928 | tf_op jit(solution)/shard_map/all_gather | solution.py:147
  523.6 5.2 reduce_sum.171
  528.8 6.0 multiply_reduce_fusion.2
  534.8 11.5 multiply_add_fusion
  546.3 10.4 multiply_convert_fusion.1
  556.8 10.6 fusion.80
  568.0 209.6 %reduce-scatter.24.cloned.1.call-done = f32[1024,768]{1,0:T(8,128)} async-done(((f32[4096,768]{1,0:T(8,128)}), f32[1024,768]{1,0:T(8,128)}) %reduce-scatter.24.cloned.1.call-update) | async-done | bytes 3145744 | tf_op jit(solution)/shard_map/reduce_scatter | solution.py:158
  777.6 3.3 fusion.78
  783.4 2.3 fusion.62
  785.8 2.7 convert_reduce_fusion.2
  788.5 116.4 %all-gather.6.cloned.1.call-done = bf16[4096,768]{1,0:T(8,128)(2,1)} async-done(((bf16[1024,768]{1,0:T(8,128)(2,1)}), bf16[4096,768]{1,0:T(8,128)(2,1)}) %all-gather.6.cloned.1.call-update) | async-done | bytes 6291472 | tf_op jit(solution)/shard_map/all_gather | solution.py:171
  905.0 13.3 convert_reduce_fusion
  918.3 2.6 copy-done.5
  920.9 8.3 fusion.81
  929.9 209.5 %reduce-scatter.26.cloned.1.call-done = f32[1024,768]{1,0:T(8,128)} async-done(((f32[4096,768]{1,0:T(8,128)}), f32[1024,768]{1,0:T(8,128)}) %reduce-scatter.26.cloned.1.call-update) | async-done | bytes 3145744 | tf_op jit(solution)/shard_map/reduce_scatter | solution.py:178
  1139.4 6.4 fusion.75
  1145.9 219.3 %all-gather.8.cloned.1.call-done = f32[4096,768]{1,0:T(8,128)} async-done(((f32[1024,768]{1,0:T(8,128)}), f32[4096,768]{1,0:T(8,128)}) %all-gather.8.cloned.1.call-update) | async-done | bytes 12582928 | tf_op jit(solution)/shard_map/all_gather | solution.py:181
  1365.2 9.9 multiply_reduce_fusion.3
  1375.1 9.7 subtract_multiply_fusion
  1384.8 4.5 copy-done.2
  1389.2 3.5 fusion.70
  1392.7 6.8 convolution_convert_fusion
  1404.8 91.0 %while.27 = (s32[]{:T(128)}, bf16[8,512,3,64]{1,3,2,0:T(8,128)(2,1)}, bf16[8,512,3,64]{1,3,2,0:T(8,128)(2,1)}, bf16[8,512,3,64]{1,3,2,0:T(8,128)(2,1)S(1)}, bf16...) while((s32[]{:T(128)}, ...), condition=%wide.region_17.18_spmd, body=%wide.region_15.17_spmd.sunk | while | flops 511146496 | bytes 26125436 | solution.py:192
  1407.4 2.2 multiply_reduce_fusion.7
  1412.0 2.2 fusion.149
  1418.8 2.2 multiply_reduce_fusion.7
  1423.4 2.2 fusion.149
  1434.7 2.2 fusion.149
  1446.0 2.2 fusion.149
  1457.4 2.2 fusion.149
  1468.7 2.2 fusion.149
  1480.1 2.2 fusion.149
  1491.4 2.2 fusion.149
  1495.8 2.3 copy.76
  1502.3 6.3 fusion.83
  1508.6 6.5 fusion.82
  1515.1 12.8 add_convert_fusion
  1527.9 11.9 fusion.66
  1539.8 10.1 fusion.84
  1550.0 4.7 convolution_bitcast_fusion.2
  1556.0 4.7 convolution_bitcast_fusion
  1563.4 4.7 convolution_bitcast_fusion.1
  1571.3 24.6 %all-reduce.3 = (f32[2,3,64]{2,1,0:T(4,128)S(1)}, f32[12,64]{1,0:T(8,128)S(1)}) all-reduce(f32[2,3,64]{2,1,0:T(4,128)S(1)} %pad_maximum_fusion, f32[12,64]{1,0:T(8,128)S(1)} %reshape.201), channel_id=12, replica_groups=mesh['dp'=8,'tensor'=4] {'dp'}, use_global_device_ids=true, to_apply=%region_27.28.clone | all-reduce | flops 1152 | bytes 9216
  1599.0 37.9 %reduce-scatter.28.cloned.1.call-done = bf16[1024,768]{1,0:T(8,128)(2,1)} async-done(((bf16[4096,768]{1,0:T(8,128)(2,1)}), bf16[1024,768]{1,0:T(8,128)(2,1)}) %reduce-scatter.28.cloned.1.call-update) | async-done | bytes 1572880 | tf_op jit(solution)/shard_map/reduce_scatter | solution.py:206
  1636.9 5.4 convert_reduce_fusion.3
  1642.4 41.1 %all-reduce.2 = f32[6,768]{1,0:T(8,128)S(1)} all-reduce(f32[6,768]{1,0:T(8,128)S(1)} %stack.39), channel_id=14, replica_groups=mesh['dp'=8,'tensor'=4] {'dp','tensor'}, use_global_device_ids=true, to_apply=%region_36.37.clone | all-reduce | flops 4608 | bytes 36864
  1684.4 46.0 %reduce-scatter.32.cloned.1.call-done = f32[768,96]{0,1:T(8,128)} async-done(((f32[768,768]{0,1:T(8,128)}), f32[768,96]{0,1:T(8,128)}) %reduce-scatter.32.cloned.1.call-update) | async-done | bytes 294928 | tf_op jit(solution)/shard_map/reduce_scatter | solution.py:218
  1730.4 38.7 %reduce-scatter.34.cloned.1.call-done = f32[96,192]{1,0:T(8,128)} async-done(((f32[768,192]{1,0:T(8,128)}), f32[96,192]{1,0:T(8,128)}) %reduce-scatter.34.cloned.1.call-update) | async-done | bytes 73744
  1769.1 38.5 %reduce-scatter.38.cloned.1.call-done = f32[96,192]{1,0:T(8,128)} async-done(((f32[768,192]{1,0:T(8,128)}), f32[96,192]{1,0:T(8,128)}) %reduce-scatter.38.cloned.1.call-update) | async-done | bytes 73744
  1807.6 38.7 %reduce-scatter.36.cloned.1.call-done = f32[96,192]{1,0:T(8,128)} async-done(((f32[768,192]{1,0:T(8,128)}), f32[96,192]{1,0:T(8,128)}) %reduce-scatter.36.cloned.1.call-update) | async-done | bytes 73744
  (251 shorter events, 135.5 us)
Async XLA Ops:
  7.2 539.1 %copy-start = (bf16[768,768]{1,0:T(8,128)(2,1)S(1)}, bf16[768,768]{1,0:T(8,128)(2,1)}, u32[]{:S(2)}) copy-start(bf16[768,768]{1,0:T(8,128)(2,1)} %param.33) | copy-start | bytes 3538948
  7.2 292.6 %reduce-scatter.22.cloned.1.call-start = ((), (), s32[]{:S(2)}) async-start(), calls=%async_computation.10 | async-start | bytes 15728640 | tf_op jit(solution)/shard_map/reduce_scatter | solution.py:139
  8.6 7.3 copy-start.17
  13.7 3.4 copy-start.13
  19.2 1.2 copy-start.15
  75.0 2.9 copy-start.8
  75.0 3.5 copy-start.12
  85.0 0.7 copy-start.23
  85.1 438.5 %all-gather.4.cloned.1.call-start = ((), (), s32[]{:S(2)}) async-start(), calls=%async_computation.11 | async-start | bytes 15728640 | tf_op jit(solution)/shard_map/all_gather | solution.py:147
  304.1 0.7 copy-start.24
  304.1 0.7 copy-start.25
  304.2 0.7 copy-start.26
  304.2 473.4 %reduce-scatter.24.cloned.1.call-start = ((), (), s32[]{:S(2)}) async-start(), calls=%async_computation.12 | async-start | bytes 15728640 | tf_op jit(solution)/shard_map/reduce_scatter | solution.py:158
  546.3 10.5 copy-start.3
  546.3 10.4 copy-start.30
  567.3 0.7 copy-start.27
  567.3 0.7 copy-start.28
  567.4 337.6 %all-gather.6.cloned.1.call-start = ((), (), s32[]{:S(2)}) async-start(), calls=%async_computation.13 | async-start | bytes 7864320 | tf_op jit(solution)/shard_map/all_gather | solution.py:171
  780.9 4.9 copy-start.4
  780.9 2.5 copy-start.6
  788.5 351.0 %reduce-scatter.26.cloned.1.call-start = ((), (), s32[]{:S(2)}) async-start(), calls=%async_computation.14 | async-start | bytes 15728640 | tf_op jit(solution)/shard_map/reduce_scatter | solution.py:178
  918.3 2.6 copy-start.5
  929.2 0.7 copy-start.29
  929.2 436.0 %all-gather.8.cloned.1.call-start = ((), (), s32[]{:S(2)}) async-start(), calls=%async_computation.15 | async-start | bytes 15728640 | tf_op jit(solution)/shard_map/all_gather | solution.py:181
  1145.8 451.5 %reduce-scatter.40.cloned.1.call-start = ((), (), s32[]{:S(2)}) async-start(), calls=%async_computation.22 | async-start | bytes 884736
  1384.8 4.5 copy-start.2
  1399.5 237.4 %reduce-scatter.28.cloned.1.call-start = ((), (), s32[]{:S(2)}) async-start(), calls=%async_computation.16 | async-start | bytes 7864320 | tf_op jit(solution)/shard_map/reduce_scatter | solution.py:206
  1498.7 3.5 copy-start.9
  1498.7 2.0 copy-start.7
  1500.3 14.8 copy-start.11
  1500.7 1.6 copy-start.16
  1502.2 6.4 copy-start.10
  1502.3 6.3 copy-start.18
  1508.6 6.5 copy-start.14
  1527.9 156.5 %reduce-scatter.30.cloned.1.call-start = ((), (), s32[]{:S(2)}) async-start(), calls=%async_computation.17 | async-start | bytes 2654208 | tf_op jit(solution)/shard_map/reduce_scatter | solution.py:217
  1539.8 190.6 %reduce-scatter.32.cloned.1.call-start = ((), (), s32[]{:S(2)}) async-start(), calls=%async_computation.18 | async-start | bytes 2654208 | tf_op jit(solution)/shard_map/reduce_scatter | solution.py:218
  1550.0 219.1 %reduce-scatter.34.cloned.1.call-start = ((), (), s32[]{:S(2)}) async-start(), calls=%async_computation.19 | async-start | bytes 884736
  1555.9 6.1 copy-start.31
  1555.9 7.3 copy-start.21
  1556.0 7.3 copy-start.20
  1556.0 7.3 copy-start.19
  1556.0 7.3 copy-start.22
  1556.0 251.6 %reduce-scatter.38.cloned.1.call-start = ((), (), s32[]{:S(2)}) async-start(), calls=%async_computation.21 | async-start | bytes 884736
  1561.9 284.3 %reduce-scatter.36.cloned.1.call-start = ((), (), s32[]{:S(2)}) async-start(), calls=%async_computation.20 | async-start | bytes 884736
  1597.3 249.0 %copy-start.1 = (bf16[768,768]{1,0:T(8,128)(2,1)S(1)}, bf16[768,768]{1,0:T(8,128)(2,1)}, u32[]{:S(2)}) copy-start(bf16[768,768]{1,0:T(8,128)(2,1)} %param.33) | copy-start | bytes 3538948
Sparse Core Ops, SparseCore 0:
  85.2 214.6 reduce-scatter.21
  304.3 219.2 all-gather.3
  567.5 210.0 reduce-scatter.23
  788.6 116.3 all-gather.5
  929.3 210.0 reduce-scatter.25
  1145.9 219.2 all-gather.7
  1399.7 33.1 reduce-scatter.39
  1528.0 108.9 reduce-scatter.27
  1640.9 43.4 reduce-scatter.29
  1688.2 42.1 reduce-scatter.31
  1734.1 34.9 reduce-scatter.33
  1772.6 34.9 reduce-scatter.37
  1811.3 34.9 reduce-scatter.35
where the time goes:
time: 1860 us; the launch traced here: 1850 us
  waiting for transfers between devices  1390 us (75%)
  matrix products  242 us (13%)
  other arithmetic  86.3 us (5%)
  blocking collectives  65.7 us (4%)
  local copies, waits for them, and re-layouts  54.6 us (3%)
    all_gather x1, waiting for transfers between devices, per_device(): lax.all_gather(grad_normed_share, 'tensor', axis=0, tiled=True)  219 us
    all_gather x1, waiting for transfers between devices, per_device(): hidden_all = lax.all_gather(hidden_share, 'tensor', axis=0, tiled=True)  219 us
    reduce_scatter x1, waiting for transfers between devices, per_device(): lax.psum_scatter(jnp.dot(picked, w_output, preferred_element_type=jnp.flo...  214 us
    reduce_scatter x1, waiting for transfers between devices, per_device(): lax.psum_scatter(jnp.dot(picked, w_project, preferred_element_type=jnp.fl...  210 us
    reduce_scatter x1, waiting for transfers between devices, per_device(): lax.psum_scatter(times_transposed(picked, w_hidden), 'tensor', scatter_di...  210 us
    all_gather x1, waiting for transfers between devices, per_device(): grad_sum_all = lax.all_gather(grad_sum_low, 'tensor', axis=0, tiled=True)  116 us
    unnamed x17, waiting for transfers between devices  116 us
    unnamed x2, blocking collectives  65.7 us
  transfers between devices with their start and end apart: 13, of which 12 were waited for; matrix products, arithmetic and copies ran while one was open for 10% of the time, Pallas kernels for 0%

commit v1 on v0

v1 whole, which is shorter than its diff:
```python
import jax
import jax.numpy as jnp
from jax import lax
from jax.sharding import PartitionSpec as P

HD = 64


norm_epsilon = 1e-12
root_half = 0.7071067811865476


def norm_forward(values, norm_gain, norm_shift):
    average = jnp.mean(values, axis=-1, keepdims=True)
    centered = values - average
    variance = jnp.mean(centered * centered, axis=-1, keepdims=True)
    inverse = lax.rsqrt(variance + norm_epsilon)
    scaled = centered * inverse
    return (scaled * norm_gain + norm_shift, scaled, inverse)


def norm_backward(grad_out, scaled, inverse, norm_gain):
    weighted = grad_out * norm_gain
    mean_grad = jnp.mean(weighted, axis=-1, keepdims=True)
    mean_proj = jnp.mean(weighted * scaled, axis=-1, keepdims=True)
    return inverse * (weighted - mean_grad - scaled * mean_proj)


def gelu_exact(values):
    return 0.5 * values * (1.0 + lax.erf(values * root_half))


def cross_rows(left, right):
    return lax.dot_general(
        left, right, (((0,), (0,)), ((), ())), preferred_element_type=jnp.float32
    )


def times_transposed(left, right):
    return lax.dot_general(
        left, right, (((1,), (1,)), ((), ())), preferred_element_type=jnp.float32
    )


def masked_scores(queries, keys_in, segment_row):
    same_text = segment_row[:, None] == segment_row[None, :]
    scores = jnp.einsum("qhd,khd->hqk", queries, keys_in, preferred_element_type=jnp.float32)
    scores = scores * queries.shape[2] ** (-0.5)
    return jnp.where(same_text[None], scores, -1000000000.0)


def attend_forward(packed):
    queries, keys_in, values, segment_row = packed
    scores = masked_scores(queries, keys_in, segment_row)
    row_max = jnp.max(scores, axis=-1, keepdims=True)
    exponent = jnp.exp(scores - row_max)
    row_total = jnp.sum(exponent, axis=-1, keepdims=True)
    attn_probs = (exponent / row_total).astype(jnp.bfloat16)
    mixed_heads = jnp.einsum("hqk,khd->qhd", attn_probs, values, preferred_element_type=jnp.float32)
    return (mixed_heads.astype(jnp.bfloat16), row_max + jnp.log(row_total))


def attend_backward(packed):
    queries, keys_in, values, segment_row, logsum, grad_mixed = packed
    score_scale = queries.shape[2] ** (-0.5)
    scores = masked_scores(queries, keys_in, segment_row)
    attn_probs = jnp.exp(scores - logsum)
    grad_probs = jnp.einsum("qhd,khd->hqk", grad_mixed, values, preferred_element_type=jnp.float32)
    grad_values = jnp.einsum(
        "hqk,qhd->khd",
        attn_probs.astype(jnp.bfloat16),
        grad_mixed,
        preferred_element_type=jnp.float32,
    )
    inner_sum = jnp.sum(attn_probs * grad_probs, axis=-1, keepdims=True)
    grad_scores = (attn_probs * (grad_probs - inner_sum)).astype(jnp.bfloat16)
    grad_queries = (
        jnp.einsum("hqk,khd->qhd", grad_scores, keys_in, preferred_element_type=jnp.float32)
        * score_scale
    )
    grad_keys = (
        jnp.einsum("hqk,qhd->khd", grad_scores, queries, preferred_element_type=jnp.float32)
        * score_scale
    )
    return (
        grad_queries.astype(jnp.bfloat16),
        grad_keys.astype(jnp.bfloat16),
        grad_values.astype(jnp.bfloat16),
    )


def per_device(
    inputs,
    segments,
    w_query,
    w_key,
    w_value,
    b_query,
    b_value,
    w_output,
    b_output,
    gain_attn,
    shift_attn,
    w_hidden,
    b_hidden,
    w_project,
    b_project,
    gain_ffn,
    shift_ffn,
    cotangent,
):
    seq_len = segments.shape[1]
    share_tokens = cotangent.shape[0]
    share_rows = share_tokens // seq_len
    width = inputs.shape[1]
    groups, parts = lax.axis_size("tensor"), lax.axis_size("dp")
    place, part = lax.axis_index("tensor"), lax.axis_index("dp")
    everyone = ("tensor", "dp")
    low = jnp.bfloat16
    wide = jnp.float32

    def gathered(shard):
        rows = shard.shape[0] // parts
        piece = lax.dynamic_slice_in_dim(shard, part * rows, rows, 0)
        return lax.all_gather(piece, everyone, axis=0, tiled=True)

    def bias_of(shard):
        return lax.all_gather(shard, "tensor", axis=0, tiled=True).astype(wide)

    tokens = lax.dynamic_slice_in_dim(inputs, place * share_tokens, share_tokens, 0)
    rows_segments = lax.dynamic_slice_in_dim(segments, place * share_rows, share_rows, 0)
    split = w_query.shape[1]
    w_in = gathered(jnp.concatenate([w_query, w_key, w_value], axis=1))
    w_in = w_in.reshape(groups, width, 3, split).transpose(1, 2, 0, 3).reshape(width, 3 * groups * split)
    w_out = gathered(w_output)
    w_up = gathered(w_hidden).reshape(groups, width, -1).transpose(1, 0, 2).reshape(width, -1)
    w_down = gathered(w_project)
    small = bias_of(jnp.concatenate([b_query, b_value, b_hidden])).reshape(groups, -1)
    bias_query = small[:, :split].reshape(-1)
    bias_value = small[:, split : 2 * split].reshape(-1)
    bias_hidden = small[:, 2 * split :].reshape(-1)
    full = groups * split
    head_shape = (share_rows, seq_len, full // HD, HD)

    attn_gain = gain_attn.astype(wide)
    attn_shift = shift_attn.astype(wide)
    attn_bias = b_output.astype(wide)
    ffn_gain = gain_ffn.astype(wide)
    ffn_shift = shift_ffn.astype(wide)
    ffn_bias = b_project.astype(wide)
    grad_out = cotangent.astype(wide)

    projected = jnp.dot(tokens, w_in, preferred_element_type=wide)
    queries = (projected[:, :full] + bias_query).astype(low)
    keys_in = projected[:, full : 2 * full].astype(low)
    values = (projected[:, 2 * full :] + bias_value).astype(low)
    query_heads = queries.reshape(head_shape)
    key_heads = keys_in.reshape(head_shape)
    value_heads = values.reshape(head_shape)
    mixed_heads, logsum = lax.map(attend_forward, (query_heads, key_heads, value_heads, rows_segments))
    mixed = mixed_heads.reshape(share_tokens, full)
    hidden = tokens.astype(wide) + (jnp.dot(mixed, w_out, preferred_element_type=wide) + attn_bias)
    normed, scaled, inverse = norm_forward(hidden, attn_gain, attn_shift)
    normed_low = normed.astype(low)
    hidden_pre = jnp.dot(normed_low, w_up, preferred_element_type=wide) + bias_hidden
    active, gelu_pull = jax.vjp(gelu_exact, hidden_pre)
    active_low = active.astype(low)
    block_sum = normed + (jnp.dot(active_low, w_down, preferred_element_type=wide) + ffn_bias)
    output, scaled_out, inverse_out = norm_forward(block_sum, ffn_gain, ffn_shift)
    grad_sum = norm_backward(grad_out, scaled_out, inverse_out, ffn_gain)
    grad_ffn_gain = jnp.sum(grad_out * scaled_out, axis=0)
    grad_ffn_shift = jnp.sum(grad_out, axis=0)
    grad_sum_low = grad_sum.astype(low)
    grad_ffn_bias = jnp.sum(grad_sum_low.astype(wide), axis=0)
    grad_active = times_transposed(grad_sum_low, w_down)
    grad_w_down = cross_rows(grad_sum_low, active_low)
    grad_hidden_pre = gelu_pull(grad_active)[0].astype(low)
    grad_b_hidden = jnp.sum(grad_hidden_pre.astype(wide), axis=0)
    grad_w_up = cross_rows(normed_low, grad_hidden_pre)
    grad_normed = grad_sum + times_transposed(grad_hidden_pre, w_up)
    grad_hidden = norm_backward(grad_normed, scaled, inverse, attn_gain)
    grad_hidden_low = grad_hidden.astype(low)
    grad_attn_gain = jnp.sum(grad_normed * scaled, axis=0)
    grad_attn_shift = jnp.sum(grad_normed, axis=0)
    grad_attn_bias = jnp.sum(grad_hidden_low.astype(wide), axis=0)
    grad_w_out = cross_rows(grad_hidden_low, mixed)
    grad_mixed = times_transposed(grad_hidden_low, w_out).astype(low).reshape(head_shape)
    grad_q, grad_k, grad_v = lax.map(
        attend_backward, (query_heads, key_heads, value_heads, rows_segments, logsum, grad_mixed)
    )
    grad_q = grad_q.reshape(share_tokens, full)
    grad_k = grad_k.reshape(share_tokens, full)
    grad_v = grad_v.reshape(share_tokens, full)
    grad_projected = jnp.concatenate([grad_q, grad_k, grad_v], axis=1)
    grad_w_in = cross_rows(tokens, grad_projected)
    grad_b_query = jnp.sum(grad_q.astype(wide), axis=0)
    grad_b_value = jnp.sum(grad_v.astype(wide), axis=0)
    grad_input = grad_hidden + times_transposed(grad_projected, w_in)

    def scattered(grad):
        rows = grad.shape[0]
        grad = grad.reshape(rows, groups, -1).transpose(1, 0, 2).reshape(groups * rows, -1)
        return lax.psum_scatter(grad, everyone, scatter_dimension=0, tiled=True)

    sum_down = scattered(grad_w_down).T
    sum_up = scattered(grad_w_up)
    sum_out = scattered(grad_w_out).T
    sum_in = scattered(
        grad_w_in.reshape(width, 3, groups, split).transpose(0, 2, 1, 3).reshape(width, -1)
    )
    vectors = jnp.concatenate(
        [
            jnp.stack([grad_b_query, grad_b_value]).reshape(2 * groups, split),
            grad_b_hidden.reshape(-1, split),
            jnp.stack(
                [
                    grad_attn_gain,
                    grad_attn_shift,
                    grad_attn_bias,
                    grad_ffn_gain,
                    grad_ffn_shift,
                    grad_ffn_bias,
                ]
            ).reshape(-1, split),
        ],
        axis=0,
    )
    vectors = lax.psum(vectors, ("dp", "tensor"))
    bias_qv = vectors[: 2 * groups].reshape(2, groups, split // HD, HD)
    rest = vectors[2 * groups :]
    hid = bias_hidden.shape[0] // split
    bias_h = rest[:hid].reshape(groups, -1, HD)
    vec = rest[hid:].reshape(6, -1)
    piece = HD // parts
    bias_qv = lax.dynamic_slice_in_dim(bias_qv, place, 1, 1)[:, 0]
    bias_qv = lax.dynamic_slice_in_dim(bias_qv, part * piece, piece, 2)
    bias_h = lax.dynamic_slice_in_dim(bias_h, place, 1, 0)[0]
    bias_h = lax.dynamic_slice_in_dim(bias_h, part * piece, piece, 1)
    piece = width // (parts * groups)
    vec = lax.dynamic_slice_in_dim(vec, (part * groups + place) * piece, piece, 1)
    return (
        output.astype(low),
        grad_input,
        sum_in[:, :split],
        sum_in[:, split : 2 * split],
        sum_in[:, 2 * split :],
        sum_out,
        sum_up,
        sum_down,
        bias_qv,
        bias_h,
        vec,
    )


def solution(mesh):
    in_specs = (
        P("dp", None),
        P("dp", None),
        P(None, "tensor"),
        P(None, "tensor"),
        P(None, "tensor"),
        P("tensor"),
        P("tensor"),
        P("tensor", None),
        P(),
        P(),
        P(),
        P(None, "tensor"),
        P("tensor"),
        P("tensor", None),
        P(),
        P(),
        P(),
        P(("dp", "tensor"), None),
    )
    out_specs = (
        P(("dp", "tensor"), None),
        P(("dp", "tensor"), None),
        P("dp", "tensor"),
        P("dp", "tensor"),
        P("dp", "tensor"),
        P("tensor", "dp"),
        P("dp", "tensor"),
        P("tensor", "dp"),
        P(None, "tensor", "dp"),
        P("tensor", "dp"),
        P(None, ("dp", "tensor")),
    )
    return jax.shard_map(
        per_device, mesh=mesh, in_specs=in_specs, out_specs=out_specs, check_vma=False
    )
```

time: 1860 us -> 862 us (0.46)
  waiting for transfers between devices: 1390 us -> 413 us
  local copies, waits for them, and re-layouts: 54.6 us -> 174 us
  matrix products: 242 us -> 150 us
  other arithmetic: 86.3 us -> 41.7 us
    all_gather x3 -> x4, waiting for transfers between devices: 554 us -> 115 us  [gathered(): return lax.all_gather(piece, everyone, axis=0, tiled=True)]
    reduce_scatter x6 -> x2, waiting for transfers between devices: 717 us -> 281 us  [scattered(): return lax.psum_scatter(grad, everyone, scatter_dimension=0, tiled=True)]
    unnamed x17 -> x10, waiting for transfers between devices: 116 us -> 17 us
    unnamed x2 -> x0, blocking collectives: 65.7 us -> none
    reshape x1 -> x13, local copies, waits for them, and re-layouts: 0.07 us -> 47.2 us  [the longest x2 25.1 us: scattered(): grad.reshape(rows, groups, -1).transpose(1, 0, 2).reshape(groups * rows, -1)]
    psum x0 -> x1, blocking collectives: none -> 41.1 us  [per_device(): vectors = lax.psum(vectors, ('dp', 'tensor'))]
    transpose x0 -> x5, local copies, waits for them, and re-layouts: none -> 31.3 us  [the longest x2 18.7 us: scattered(): grad.reshape(rows, groups, -1).transpose(1, 0, 2).reshape(groups * rows, -1)]
    reduce_sum x8 -> x4, other arithmetic: 34.8 us -> 8.95 us  [the longest x1 3.72 us: per_device(): grad_attn_bias = jnp.sum(grad_hidden_low.astype(wide), axis=0)]
  transfers between devices with their start and end apart: 13 -> 8, of which waited for: 12 -> 6; matrix products, arithmetic and copies ran while one was open for 10% -> 34% of each run, Pallas kernels for 0% -> 0%
where the time goes in v1:
time: 862 us; the launch traced here: 852 us
  waiting for transfers between devices  413 us (48%)
  local copies, waits for them, and re-layouts  174 us (20%)
  matrix products  150 us (17%)
  blocking collectives  56.1 us (7%)
  other arithmetic  41.7 us (5%)
  between operations  15 us (2%)
    reduce_scatter x2, waiting for transfers between devices, scattered(): return lax.psum_scatter(grad, everyone, scatter_dimension=0, tiled=True)  281 us
    all_gather x4, waiting for transfers between devices, gathered(): return lax.all_gather(piece, everyone, axis=0, tiled=True)  115 us
    psum x1, blocking collectives, per_device(): vectors = lax.psum(vectors, ('dp', 'tensor'))  41.1 us
    dot_general x4, matrix products, times_transposed(): lax.dot_general(left, right, (((1,), (1,)), ((), ())), preferred_element_...  38.8 us
    unnamed x103, local copies, waits for them, and re-layouts  38.6 us
    dot_general x4, matrix products, cross_rows(): lax.dot_general(left, right, (((0,), (0,)), ((), ())), preferred_element_...  28.9 us
    reshape x2, local copies, waits for them, and re-layouts, scattered(): grad.reshape(rows, groups, -1).transpose(1, 0, 2).reshape(groups * rows, -1)  25.1 us
    transpose x2, local copies, waits for them, and re-layouts, scattered(): grad.reshape(rows, groups, -1).transpose(1, 0, 2).reshape(groups * rows, -1)  18.7 us
  transfers between devices with their start and end apart: 8, of which 6 were waited for; matrix products, arithmetic and copies ran while one was open for 34% of the time, Pallas kernels for 0%

profile of v1, /device:TPU:0, one launch (start us, length us, event | category | flops | bytes accessed | tf_op | source)
XLA Modules:
  0.0 851.7 jit_solution(8184249609554273054)
XLA Ops:
  18.6 14.9 %all-gather = bf16[4,1,1152]{2,1,0:T(2,128)(2,1)S(1)} all-gather(bf16[1,1,1152]{2,1,0:T(2,128)(2,1)S(1)} %reshape.275), channel_id=1, replica_groups=mesh['dp'=8,'tensor'=4] {'tensor'}, dimensions={0}, use_global_device_ids=true | all-gather | bytes 11520 | tf_op jit(solution)/shard_map/all_gather | solution.py:128
  45.4 31.5 %all-gather.6.cloned.1.call-done = bf16[3072,576]{1,0:T(8,128)(2,1)} async-done(((bf16[96,576]{1,0:T(8,128)(2,1)}), bf16[3072,576]{1,0:T(8,128)(2,1)}) %all-gather.6.cloned.1.call-update) | async-done | bytes 3538960 | tf_op jit(solution)/shard_map/all_gather | solution.py:125
  76.9 6.0 copy.132
  82.9 7.7 reshape.246
  90.6 2.5 copy.133
  93.2 3.9 fusion.82
  102.4 2.4 reshape.251
  106.5 2.6 copy.136
  109.1 3.9 reshape.252
  113.0 2.9 copy.139
  115.8 2.6 copy.134
  118.4 3.9 reshape.250
  122.3 2.9 copy.137
  126.5 23.3 %while.26 = (s32[]{:T(128)}, bf16[2,512,12,64]{1,3,2,0:T(8,128)(2,1)}, f32[2,12,512,1]{2,1,3,0:T(8,128)S(1)}, bf16[2,512,12,64]{1,3,2,0:T(8,128)(2,1)}, s32[2,51...) while((s32[]{:T(128)}, ...), condition=%wide.region_3.4_spmd, body=%wide.region_0.3_spmd.sunk | while | flops 843704320 | bytes 42172516 | solution.py:160
  126.9 3.2 fusion.124
  130.1 2.6 fusion.125
  132.7 5.5 fusion.126
  138.4 3.2 fusion.124
  141.7 2.6 fusion.125
  144.2 5.5 fusion.126
  149.8 3.0 copy.140
  154.4 3.9 fusion.80
  160.4 38.9 %all-gather.10.cloned.1.call-done = bf16[3072,768]{1,0:T(8,128)(2,1)} async-done(((bf16[96,768]{1,0:T(8,128)(2,1)}), bf16[3072,768]{1,0:T(8,128)(2,1)}) %all-gather.10.cloned.1.call-update) | async-done | bytes 4718608 | tf_op jit(solution)/shard_map/all_gather | solution.py:125
  199.2 6.8 copy.141
  206.0 13.9 %multiply_convert_fusion.3 = (bf16[1024,3072]{1,0:T(8,128)(2,1)}, f32[1024,3072]{1,0:T(8,128)}) fusion(f32[3072]{0:T(1024)S(1)} %copy-done.34, bf16[768,3072]{0,1:T(8,128)(2,1)} %bitcast.212, f32[1024,768]{0,1:T(8,128)} %copy-done.9, f32[768]{0:T(1024)S(1)} %copy-done.37, f32[768]{0:T(1024)S(1)} %copy-done.26, f32[1024]{0:T(1024)S(1)} %add_rsqrt_fusion.1, ...), kind=kOutput, calls=%fused_computation.66 | convolution fusion | flops 4854644736 | bytes 26765312 | tf_op jit(solution)/shard_map/dot_general | solution.py:165
  219.9 44.6 %all-gather.12.cloned.1.call-done = bf16[3072,768]{1,0:T(8,128)(2,1)} async-done(((bf16[96,768]{1,0:T(8,128)(2,1)}), bf16[3072,768]{1,0:T(8,128)(2,1)}) %all-gather.12.cloned.1.call-update) | async-done | bytes 4718608 | tf_op jit(solution)/shard_map/all_gather | solution.py:125
  264.5 9.4 %fusion.81 = (f32[1024]{0:T(1024)S(1)}, f32[1024,768]{0,1:T(8,128)S(1)}) fusion(f32[768]{0:T(1024)S(1)} %copy-done.39, bf16[1024,3072]{1,0:T(8,128)(2,1)} %get-tuple-element.280, bf16[3072,768]{1,0:T(8,128)(2,1)} %all-gather.12.cloned.1.call-done, f32[768]{0:T(1024)S(1)} %copy-done.37, f32[768]{0:T(1024)S(1)} %copy-done.26, f32[1024]{0:T(1024)S(1)} %add_rsqrt_fusion.1, ...), kind=kOutput, calls=%fused_computation.141 | convolution fusion | flops 4837342208 | bytes 17323008 | tf_op jit(solution)/shard_map/dot_general | solution.py:168
  277.3 3.3 convert_reduce_fusion.2
  280.6 15.3 %convert_reduce_fusion = (f32[3072]{0:T(1024)}, bf16[1024,3072]{1,0:T(8,128)(2,1)}) fusion(bf16[1024,768]{0,1:T(8,128)(2,1)S(1)} %get-tuple-element.263, bf16[3072,768]{1,0:T(8,128)(2,1)S(1)} %copy-done.45, f32[1024,3072]{1,0:T(8,128)} %get-tuple-element.281, f32[3072]{0:T(1024)S(1)} %copy-done.34), kind=kOutput, calls=%fused_computation.64 | convolution fusion | flops 4882166784 | bytes 25190400 | tf_op jit(solution)/shard_map/dot_general | solution.py:40
  295.9 11.0 %multiply_reduce_fusion.1 = (f32[768]{0:T(1024)}, f32[1024]{0:T(1024)S(1)}, f32[1024]{0:T(1024)S(1)}, f32[768]{0:T(1024)}, f32[1024,768]{0,1:T(8,128)}) fusion(f32[1024,768]{0,1:T(8,128)S(1)} %copy-done.10, f32[1024]{0:T(1024)S(1)} %add_rsqrt_fusion.1, f32[1024]{0:T(1024)S(1)} %broadcast_multiply_fusion.5, f32[768]{0:T(1024)S(1)} %copy-done.26, ...), kind=kOutput, calls=%fused_computation.85 | convolution fusion | flops 4845989888 | bytes 22065152 | tf_op jit(solution)/shard_map/dot_general | solution.py:40
  306.9 3.7 convert_reduce_fusion.3
  312.4 2.6 convolution_convert_fusion
  315.0 2.6 copy.145
  317.6 3.8 reshape.256
  321.4 3.1 copy.148
  324.5 4.3 convolution_bitcast_fusion
  328.8 3.4 copy.183
  336.2 52.2 %while.27 = (s32[]{:T(128)}, bf16[2,512,12,64]{1,3,2,0:T(8,128)(2,1)}, bf16[2,512,12,64]{1,3,2,0:T(8,128)(2,1)}, bf16[2,512,12,64]{1,3,2,0:T(8,128)(2,1)}, bf16[...) while((s32[]{:T(128)}, ...), condition=%wide.region_14.15_spmd, body=%wide.region_12.14_spmd.sunk | while | flops 2062673920 | bytes 147524944 | solution.py:188
  336.7 3.1 fusion.135
  339.8 3.9 fusion.138
  343.8 6.8 multiply_reduce_fusion.7
  350.6 7.3 multiply_convert_fusion.5
  362.5 3.1 fusion.135
  365.6 4.0 fusion.138
  369.6 6.8 multiply_reduce_fusion.7
  376.5 7.2 multiply_convert_fusion.5
  388.4 3.1 copy.151
  391.9 3.2 copy.152
  399.1 3.9 fusion.84
  403.0 3.3 copy.155
  406.4 8.4 copy.182
  415.5 10.8 %fusion.73 = f32[768,3072]{1,0:T(8,128)} fusion(bf16[1024,3072]{1,0:T(8,128)(2,1)} %get-tuple-element.286, f32[1024,768]{0,1:T(8,128)} %copy-done.9, f32[768]{0:T(1024)S(1)} %copy-done.38, f32[768]{0:T(1024)S(1)} %copy-done.27, f32[1024]{0:T(1024)S(1)} %copy-done.29, f32[1024]{0:T(1024)S(1)} %copy-done.22), kind=kOutput, calls=%fused_computation.136 | convolution fusion | flops 4835770368 | bytes 18888704 | tf_op jit(solution)/shard_map/dot_general | solution.py:34
  426.2 12.5 %reshape.263 = f32[768,4,768]{2,1,0:T(4,128)} reshape(f32[768,3072]{1,0:T(8,128)} %fusion.73) | data formatting | bytes 18874368 | tf_op jit(solution)/shard_map/reshape | solution.py:202
  438.7 9.2 %copy.159 = f32[4,768,768]{2,1,0:T(8,128)} copy(f32[4,768,768]{2,0,1:T(4,128)} %bitcast.197) | data formatting | bytes 18874368 | tf_op jit(solution)/shard_map/transpose | solution.py:202
  447.9 10.0 %fusion.83 = f32[768,3072]{1,0:T(8,128)} fusion(bf16[1024,768]{0,1:T(8,128)(2,1)} %copy-done.19, bf16[1024,3072]{1,0:T(8,128)(2,1)} %get-tuple-element.280), kind=kOutput, calls=%fused_computation.143 | convolution fusion | flops 4831838208 | bytes 17301504 | tf_op jit(solution)/shard_map/dot_general | solution.py:34
  457.9 12.7 %reshape.265 = f32[768,4,768]{2,1,0:T(4,128)} reshape(f32[768,3072]{1,0:T(8,128)} %fusion.83) | data formatting | bytes 18874368 | tf_op jit(solution)/shard_map/reshape | solution.py:202
  470.6 9.5 %copy.160 = f32[4,768,768]{2,1,0:T(8,128)} copy(f32[4,768,768]{2,0,1:T(4,128)} %bitcast.198) | data formatting | bytes 18874368 | tf_op jit(solution)/shard_map/transpose | solution.py:202
  483.4 41.1 %psum.7 = f32[48,192]{1,0:T(8,128)S(1)} all-reduce(f32[48,192]{1,0:T(8,128)S(1)} %pad_maximum_fusion), channel_id=1, replica_groups=mesh['dp'=8,'tensor'=4] {'dp','tensor'}, use_global_device_ids=true, to_apply=%region_28.29 | all-reduce | flops 9216 | bytes 73728 | tf_op jit(solution)/shard_map/psum | solution.py:228
  526.2 2.6 copy.163
  528.7 10.0 %convolution_add_fusion.1 = f32[1024,768]{0,1:T(8,128)} fusion(f32[1024,768]{0,1:T(8,128)} %copy-done.16, bf16[1024,2304]{0,1:T(8,128)(2,1)} %copy-done.20, bf16[768,2304]{0,1:T(8,128)(2,1)} %bitcast.217), kind=kOutput, calls=%fused_computation.101 | convolution fusion | flops 3624665088 | bytes 14548992 | tf_op jit(solution)/shard_map/dot_general | solution.py:40
  538.7 3.5 copy.164
  544.6 16.9 %reduce-scatter.13.cloned.1.call-done = f32[96,576]{1,0:T(8,128)} async-done(((f32[3072,576]{1,0:T(8,128)}), f32[96,576]{1,0:T(8,128)}) %reduce-scatter.13.cloned.1.call-update) | async-done | bytes 221200
  563.3 139.7 %reduce-scatter.9.cloned.1.call-done = f32[96,768]{1,0:T(8,128)} async-done(((f32[3072,768]{1,0:T(8,128)}), f32[96,768]{1,0:T(8,128)}) %reduce-scatter.9.cloned.1.call-update) | async-done | bytes 294928 | tf_op jit(solution)/shard_map/reduce_scatter | solution.py:203
  703.0 141.7 %reduce-scatter.11.cloned.1.call-done = f32[96,768]{1,0:T(8,128)} async-done(((f32[3072,768]{1,0:T(8,128)}), f32[96,768]{1,0:T(8,128)}) %reduce-scatter.11.cloned.1.call-update) | async-done | bytes 294928 | tf_op jit(solution)/shard_map/reduce_scatter | solution.py:203
  (228 shorter events, 67.8 us)
Async XLA Ops:
  7.2 7.5 copy-start
  7.2 9.9 %copy-start.41 = (bf16[768]{0:T(1024)(128)(2,1)S(1)}, bf16[768]{0:T(1024)(128)(2,1)}, u32[]{:S(2)}) copy-start(bf16[768]{0:T(1024)(128)(2,1)} %param.34) | copy-start | bytes 4612
  7.2 26.3 %copy-start.42 = (bf16[768]{0:T(1024)(128)(2,1)S(1)}, bf16[768]{0:T(1024)(128)(2,1)}, u32[]{:S(2)}) copy-start(bf16[768]{0:T(1024)(128)(2,1)} %param.31) | copy-start | bytes 4612
  7.2 26.9 %copy-start.43 = (bf16[768]{0:T(1024)(128)(2,1)S(1)}, bf16[768]{0:T(1024)(128)(2,1)}, u32[]{:S(2)}) copy-start(bf16[768]{0:T(1024)(128)(2,1)} %param.32) | copy-start | bytes 4612
  7.2 27.5 %copy-start.44 = (bf16[768]{0:T(1024)(128)(2,1)S(1)}, bf16[768]{0:T(1024)(128)(2,1)}, u32[]{:S(2)}) copy-start(bf16[768]{0:T(1024)(128)(2,1)} %param.37) | copy-start | bytes 4612
  7.2 32.7 %copy-start.18 = (bf16[1024,768]{1,0:T(8,128)(2,1)S(1)}, bf16[1024,768]{1,0:T(8,128)(2,1)}, u32[]{:S(2)}) copy-start(bf16[1024,768]{1,0:T(8,128)(2,1)} %param.39) | copy-start | bytes 4718596
  7.2 69.7 %all-gather.6.cloned.1.call-start = ((), (), s32[]{:S(2)}) async-start(), calls=%async_computation.4 | async-start | bytes 4055040 | tf_op jit(solution)/shard_map/all_gather | solution.py:125
  13.2 141.2 %all-gather.8.cloned.1.call-start = ((), (), s32[]{:S(2)}) async-start(), calls=%async_computation.5 | async-start | bytes 1216512 | tf_op jit(solution)/shard_map/all_gather | solution.py:125
  14.6 184.6 %all-gather.10.cloned.1.call-start = ((), (), s32[]{:S(2)}) async-start(), calls=%async_computation.6 | async-start | bytes 4866048 | tf_op jit(solution)/shard_map/all_gather | solution.py:125
  15.4 249.1 %all-gather.12.cloned.1.call-start = ((), (), s32[]{:S(2)}) async-start(), calls=%async_computation.7 | async-start | bytes 4866048 | tf_op jit(solution)/shard_map/all_gather | solution.py:125
  17.1 525.9 %reduce-scatter.15.cloned.1.call-start = ((), (), s32[]{:S(2)}) async-start(), calls=%async_computation.11 | async-start | bytes 3244032
  43.1 50.1 %copy-start.13 = (bf16[1024,768]{1,0:T(8,128)(2,1)}, bf16[1024,768]{1,0:T(8,128)(2,1)S(1)}, u32[]{:S(2)}) copy-start(bf16[1024,768]{1,0:T(8,128)(2,1)S(1)} %constant_dynamic-slice_fusion.9) | copy-start | bytes 4718596
  93.2 3.9 copy-start.15
  149.7 4.6 copy-start.40
  158.3 1.7 copy-start.9
  158.3 148.6 %copy-start.21 = (f32[1024]{0:T(1024)}, f32[1024]{0:T(1024)S(1)}, u32[]{:S(2)}) copy-start(f32[1024]{0:T(1024)S(1)} %broadcast_multiply_fusion.5) | copy-start | bytes 12292
  160.4 146.5 %copy-start.28 = (f32[1024]{0:T(1024)}, f32[1024]{0:T(1024)S(1)}, u32[]{:S(2)}) copy-start(f32[1024]{0:T(1024)S(1)} %add_rsqrt_fusion.1) | copy-start | bytes 12292
  199.2 6.8 copy-start.26
  199.2 6.8 copy-start.34
  199.2 6.8 copy-start.37
  206.0 58.5 %copy-start.39 = (f32[768]{0:T(1024)S(1)}, f32[768]{0:T(1024)}, u32[]{:S(2)}) copy-start(f32[768]{0:T(1024)} %convert_element_type.111) | copy-start | bytes 9220
  273.9 1.4 copy-start.8
  273.9 1.4 copy-start.23
  274.4 3.0 copy-start.30
  275.3 5.2 copy-start.45
  277.3 18.5 %slice-start = ((s8[4718592]{0:T(1024)(128)(4,1)}), s8[4194304]{0:T(1024)(128)(4,1)S(1)}, s32[]{:S(2)}) async-start(s8[4718592]{0:T(1024)(128)(4,1)} %bitcast.213), calls=%async_computation.12 | async-start | bytes 8388608
  280.6 15.3 %copy-start.19 = (bf16[1024,768]{0,1:T(8,128)(2,1)}, bf16[1024,768]{0,1:T(8,128)(2,1)S(1)}, u32[]{:S(2)}) copy-start(bf16[1024,768]{0,1:T(8,128)(2,1)S(1)} %get-tuple-element.263) | copy-start | bytes 4718596
  280.6 15.3 %copy-start.10 = (f32[1024,768]{0,1:T(8,128)S(1)}, f32[1024,768]{0,1:T(8,128)}, u32[]{:S(2)}) copy-start(f32[1024,768]{0,1:T(8,128)} %copy-done.9) | copy-start | bytes 9437188
  280.6 15.3 %slice-start.1 = ((s8[4718592]{0:T(1024)(128)(4,1)}), s8[524288]{0:T(1024)(128)(4,1)S(1)}, s32[]{:S(2)}) async-start(s8[4718592]{0:T(1024)(128)(4,1)} %bitcast.213), calls=%async_computation.13 | async-start | bytes 1048576
  306.9 5.5 copy-start.46
  310.6 1.7 copy-start.16
  321.4 3.1 copy-start.17
  332.2 229.3 %reduce-scatter.13.cloned.1.call-start = ((), (), s32[]{:S(2)}) async-start(), calls=%async_computation.10 | async-start | bytes 8110080
  336.7 3.1 copy-start.4
  339.8 4.0 copy-start.3
  350.6 7.3 copy-start.11
  357.9 2.0 copy-start.2
  357.9 2.0 copy-start.5
  360.0 1.2 copy-start.12
  361.1 1.1 copy-start.6
  362.5 3.1 copy-start.4
  365.6 4.0 copy-start.3
  376.5 7.2 copy-start.11
  383.7 2.0 copy-start.2
  383.7 2.0 copy-start.5
  385.7 1.1 copy-start.12
  386.9 1.1 copy-start.6
  391.9 3.6 copy-start.7
  397.7 1.4 copy-start.14
  399.1 3.9 copy-start.20
  414.8 0.7 copy-start.22
  414.8 0.7 copy-start.27
  414.8 0.7 copy-start.29
  414.8 0.7 copy-start.38
  414.8 288.2 %reduce-scatter.9.cloned.1.call-start = ((), (), s32[]{:S(2)}) async-start(), calls=%async_computation.8 | async-start | bytes 9732096 | tf_op jit(solution)/shard_map/reduce_scatter | solution.py:203
  447.9 396.8 %reduce-scatter.11.cloned.1.call-start = ((), (), s32[]{:S(2)}) async-start(), calls=%async_computation.9 | async-start | bytes 9732096 | tf_op jit(solution)/shard_map/reduce_scatter | solution.py:203
  480.1 0.7 copy-start.32
  480.1 0.7 copy-start.31
  480.1 0.7 copy-start.36
  480.1 0.7 copy-start.24
  480.1 0.7 copy-start.35
  480.1 0.8 copy-start.25
  480.2 0.8 copy-start.33
  528.7 315.9 %copy-start.1 = (bf16[768,768]{1,0:T(8,128)(2,1)S(1)}, bf16[768,768]{1,0:T(8,128)(2,1)}, u32[]{:S(2)}) copy-start(bf16[768,768]{1,0:T(8,128)(2,1)} %param.33) | copy-start | bytes 3538948
Sparse Core Ops, SparseCore 0:
  13.3 63.5 all-gather.5
  80.4 52.7 all-gather.7
  136.7 62.4 all-gather.9
  202.5 61.9 all-gather.11
  332.4 100.4 reduce-scatter.14
  438.4 123.0 reduce-scatter.12
  568.0 135.0 reduce-scatter.8
  709.5 135.1 reduce-scatter.10
